TPU v7x, 32 devices: a whole 2x2x4 slice. The times are simulated.
32 devices in a mesh: seq: 4 (over y, x), ep: 8 (over z, core).
Axes of the slice: x: 2, y: 2, z: 4, core: 2. Of those that a mesh axis runs over, the one named last changes fastest.
Arguments:
- tokens: bfloat16 [24, 576, 768], P('ep', 'seq'), may hold values from -6 to 6
- routes: int32 [24, 576, 2], P('ep', 'seq'), may hold values from 0 to 31, all different within a row
- priority: int32 [24, 576], P('ep', 'seq'), may hold values from 0 to 431, as said below
- hires: int32 [8], P('ep'), may hold values from 0 to 3
- gain_one: float32 [768], replicated, may hold values from 0.1 to 1.9
- shift_one: float32 [768], replicated, may hold values from -1.8 to 1.8
- w_qkv: bfloat16 [768, 2304], replicated, may hold values from -0.21875 to 0.21875
- w_proj: bfloat16 [768, 768], replicated, may hold values from -6 to 6
- gain_two: float32 [768], replicated, may hold values from 0.1 to 1.9
- shift_two: float32 [768], replicated, may hold values from -1.8 to 1.8
- w_router: bfloat16 [768, 32], replicated, may hold values from -0.15917969 to 0.15917969
- expert_in: bfloat16 [98304, 768], P('ep'), may hold values from -0.21875 to 0.21875
- expert_out: bfloat16 [98304, 768], P('ep'), may hold values from -2.5 to 2.5
- cotangent: bfloat16 [24, 576, 768], P('ep', 'seq'), may hold values from -6 to 6
Outputs:
- output: bfloat16 [24, 576, 768], P('ep', 'seq')
- input_grad: bfloat16 [24, 576, 768], P('ep', 'seq')
- gain_one_grad: float32 [768], replicated
- shift_one_grad: float32 [768], replicated
- qkv_grad: float32 [768, 2304], replicated
- proj_grad: float32 [768, 768], replicated
- gain_two_grad: float32 [768], replicated
- shift_two_grad: float32 [768], replicated
- router_grad: float32 [768, 32], replicated
- expert_in_grad: float32 [98304, 768], P('ep')
- expert_out_grad: float32 [98304, 768], P('ep')
- rms_stats: float32 [3], replicated
Inputs may be any that keep to these rules, and one draw needn't show every extreme that they name: `priority`: within each device block of 3 images times 144 positions, the priorities are a permutation of 0 to 431.
All inputs are finite; a program needn't handle non-finite values.
Results may differ from a plain program's by a relative error of at most 0.015.
Values may be sent and summed in bfloat16 or wider, within the bound.
No kernel may reach another device: no remote copies, remote signals or barrier semaphores. Data moves between devices by JAX's collectives and lax.ppermute only.
A program may use at most 320 MiB of HBM per device.

v0:
```python
import jax
import jax.numpy as jnp
from jax import lax
from jax.sharding import PartitionSpec as P

HEADS = 12
EXPERTS = 32
TOP = 2
PATCHES = 576
SHORT = 196
norm_eps = 1e-06
neg_big = -1e30


def norm_forward(values, norm_gain, norm_bias):
    row_mean = jnp.mean(values, axis=-1, keepdims=True)
    centred = values - row_mean
    inv_root = lax.rsqrt(jnp.mean(centred * centred, axis=-1, keepdims=True) + norm_eps)
    normed = centred * inv_root
    return (normed * norm_gain + norm_bias, normed, inv_root)


def norm_backward(grad_out, normed, inv_root, norm_gain):
    gain_grad = jnp.sum(grad_out * normed, axis=0)
    bias_grad = jnp.sum(grad_out, axis=0)
    scaled = grad_out * norm_gain
    grad_in = inv_root * (
        scaled
        - jnp.mean(scaled, axis=-1, keepdims=True)
        - normed * jnp.mean(scaled * normed, axis=-1, keepdims=True)
    )
    return (grad_in, gain_grad, bias_grad)


def gelu_slope(values):
    return (
        0.5 * (1.0 + lax.erf(values * 0.7071067811865476))
        + values * jnp.exp(-0.5 * values * values) * 0.3989422804014327
    )


def routing(route_rows, priority_rows, row_valid, capacity):
    row_total = route_rows.shape[0]
    by_priority = (
        jnp.zeros((row_total,), jnp.int32)
        .at[priority_rows]
        .set(jnp.arange(row_total, dtype=jnp.int32))
    )
    ordered = jnp.concatenate([route_rows[by_priority, route_rank] for route_rank in range(TOP)])
    ordered_valid = jnp.concatenate([row_valid[by_priority]] * TOP)
    expert_hits = (
        ordered[:, None] == jnp.arange(EXPERTS, dtype=jnp.int32)[None, :]
    ) & ordered_valid[:, None]
    running = jnp.cumsum(expert_hits.astype(jnp.int32), axis=0)
    ordered_slot = jnp.sum(jnp.where(expert_hits, running, 0), axis=1) - 1
    pair_slot = ordered_slot.reshape(TOP, row_total)[:, priority_rows].T
    is_kept = (pair_slot >= 0) & (pair_slot < capacity)
    return jnp.where(is_kept, route_rows * capacity + pair_slot, EXPERTS * capacity)


def slot_sources(slot_dest, fill_value, capacity, divisor):
    flat_dest = slot_dest.reshape(-1)
    source_ids = jnp.arange(flat_dest.shape[0], dtype=jnp.int32) // divisor
    table_ids = (
        jnp.full((EXPERTS * capacity + 1,), fill_value, jnp.int32).at[flat_dest].set(source_ids)
    )
    return table_ids[: EXPERTS * capacity]


def fan_out(slot_table, ep_count, split_count, local_experts, capacity):
    feature_width = slot_table.shape[-1]
    grouped = slot_table.reshape(ep_count // split_count, 1, local_experts, capacity, feature_width)
    spread = jnp.broadcast_to(
        grouped, (ep_count // split_count, split_count, local_experts, capacity, feature_width)
    )
    return spread.reshape(ep_count, local_experts, capacity, feature_width)


def fan_in(arrived, split_count):
    ep_count, local_experts, capacity, feature_width = arrived.shape
    grouped = arrived.reshape(
        ep_count // split_count, split_count, local_experts, capacity, feature_width
    )
    return jnp.sum(grouped.astype(jnp.float32), axis=1).reshape(-1, feature_width)


def score_block(query_heads, key_heads, key_mask, score_scale):
    raw_scores = (
        jnp.einsum("ishd,ithd->ihst", query_heads, key_heads, preferred_element_type=jnp.float32)
        * score_scale
    )
    return jnp.where(key_mask[:, None, None, :], raw_scores, neg_big)


def per_device(
    tokens,
    routes,
    priority,
    hires,
    gain_one,
    shift_one,
    w_qkv,
    w_proj,
    gain_two,
    shift_two,
    w_router,
    expert_in,
    expert_out,
    cotangent,
):
    image_count, patch_rows, model_width = tokens.shape
    row_count = image_count * patch_rows
    seq_count = lax.axis_size("seq")
    ep_count = lax.axis_size("ep")
    full_patches = patch_rows * seq_count
    head_width = model_width // HEADS
    score_scale = head_width ** (-0.5)
    local_experts = max(1, EXPERTS // ep_count)
    split_count = max(1, ep_count // EXPERTS)
    local_hidden = expert_in.shape[0] // local_experts
    capacity = max(2, (105 * TOP * row_count + 100 * EXPERTS - 1) // (100 * EXPERTS))
    seq_place = lax.axis_index("seq")

    def send_slots(slot_table):
        outgoing = fan_out(slot_table, ep_count, split_count, local_experts, capacity)
        return lax.all_to_all(outgoing, "ep", split_axis=0, concat_axis=0, tiled=True)

    def return_slots(part_rows):
        returned = lax.all_to_all(part_rows, "ep", split_axis=0, concat_axis=0, tiled=True)
        return fan_in(returned, split_count)

    image_length = jnp.where(jnp.arange(image_count, dtype=jnp.int32) < hires[0], PATCHES, SHORT)
    key_mask = jnp.arange(full_patches, dtype=jnp.int32)[None, :] < image_length[:, None]
    own_mask = (seq_place * patch_rows + jnp.arange(patch_rows, dtype=jnp.int32))[
        None, :
    ] < image_length[:, None]
    row_valid = own_mask.reshape(row_count)
    valid_col = row_valid.astype(jnp.float32)[:, None]
    inputs = tokens.reshape(row_count, model_width).astype(jnp.float32)
    head_shape = (image_count, -1, HEADS, head_width)
    first_out, normed_one, inv_one = norm_forward(inputs, gain_one, shift_one)
    attn_in = first_out.astype(jnp.bfloat16)
    packed = jnp.dot(attn_in, w_qkv, preferred_element_type=jnp.float32).astype(jnp.bfloat16)
    query_rows = packed[:, :model_width].reshape(image_count, patch_rows, model_width)
    key_rows = packed[:, model_width : 2 * model_width].reshape(
        image_count, patch_rows, model_width
    )
    value_rows = packed[:, 2 * model_width :].reshape(image_count, patch_rows, model_width)
    query_heads = query_rows.reshape(head_shape)
    keys_all, values_all = (
        lax.all_gather(key_rows, "seq", axis=1, tiled=True),
        lax.all_gather(value_rows, "seq", axis=1, tiled=True),
    )
    scores = score_block(query_heads, keys_all.reshape(head_shape), key_mask, score_scale)
    row_max = jnp.max(scores, axis=-1, keepdims=True)
    exp_scores = jnp.exp(scores - row_max)
    row_total = jnp.sum(exp_scores, axis=-1, keepdims=True)
    probs = exp_scores / row_total
    log_total = row_max + jnp.log(row_total)
    attended = (
        jnp.einsum(
            "ihst,ithd->ishd",
            probs.astype(jnp.bfloat16),
            values_all.reshape(head_shape),
            preferred_element_type=jnp.float32,
        )
        .reshape(row_count, model_width)
        .astype(jnp.bfloat16)
    )
    attn_out = jnp.dot(attended, w_proj, preferred_element_type=jnp.float32)
    middle = inputs + attn_out
    second_out, normed_two, inv_two = norm_forward(middle, gain_two, shift_two)
    moe_in = second_out.astype(jnp.bfloat16)
    logits = jnp.dot(moe_in, w_router, preferred_element_type=jnp.float32)
    gate_probs = jax.nn.softmax(logits, axis=-1)
    route_rows = routes.reshape(row_count, TOP)
    slot_dest = routing(route_rows, priority.reshape(row_count), row_valid, capacity)
    token_src = slot_sources(slot_dest, row_count, capacity, TOP)
    pair_src = slot_sources(slot_dest, row_count * TOP, capacity, 1)
    padded_in = jnp.concatenate([moe_in, jnp.zeros((1, model_width), jnp.bfloat16)], axis=0)
    arrived = send_slots(padded_in[token_src])
    w_first = expert_in.reshape(local_experts, local_hidden, model_width)
    w_second = expert_out.reshape(local_experts, local_hidden, model_width)
    pre_act = jnp.einsum("secd,efd->secf", arrived, w_first, preferred_element_type=jnp.float32)
    hidden = jax.nn.gelu(pre_act, approximate=False).astype(jnp.bfloat16)
    partial_out = jnp.einsum(
        "secf,efd->secd", hidden, w_second, preferred_element_type=jnp.float32
    ).astype(jnp.bfloat16)
    value_table = return_slots(partial_out)
    padded_values = jnp.concatenate([value_table, jnp.zeros((1, model_width), jnp.float32)], axis=0)
    pair_values = padded_values[slot_dest.reshape(-1)].reshape(row_count, TOP, model_width)
    chosen = jnp.take_along_axis(gate_probs, route_rows, axis=1)
    moe_out = jnp.sum(chosen[:, :, None] * pair_values, axis=1)
    total = middle + moe_out
    output = (total * valid_col).astype(jnp.bfloat16).reshape(image_count, patch_rows, model_width)
    stat_terms = jnp.stack(
        [
            jnp.sum(valid_col * attn_out * attn_out),
            jnp.sum(valid_col * moe_out * moe_out),
            jnp.sum(valid_col * total * total),
            jnp.sum(row_valid.astype(jnp.float32)) * model_width,
        ]
    )
    grad_total = cotangent.reshape(row_count, model_width).astype(jnp.float32) * valid_col
    grad_gate = jnp.sum(grad_total[:, None, :] * pair_values, axis=2)
    grad_value = (
        (grad_total[:, None, :] * chosen[:, :, None])
        .astype(jnp.bfloat16)
        .reshape(row_count * TOP, model_width)
    )
    padded_grad = jnp.concatenate([grad_value, jnp.zeros((1, model_width), jnp.bfloat16)], axis=0)
    grad_sent = send_slots(padded_grad[pair_src])
    grad_hidden = jnp.einsum(
        "secd,efd->secf", grad_sent, w_second, preferred_element_type=jnp.float32
    )
    grad_pre = (grad_hidden * gelu_slope(pre_act)).astype(jnp.bfloat16)
    grad_second = jnp.einsum(
        "secf,secd->efd", hidden, grad_sent, preferred_element_type=jnp.float32
    ).reshape(-1, model_width)
    grad_first = jnp.einsum(
        "secf,secd->efd", grad_pre, arrived, preferred_element_type=jnp.float32
    ).reshape(-1, model_width)
    grad_part_in = jnp.einsum(
        "secf,efd->secd", grad_pre, w_first, preferred_element_type=jnp.float32
    ).astype(jnp.bfloat16)
    grad_in_table = return_slots(grad_part_in)
    padded_back = jnp.concatenate([grad_in_table, jnp.zeros((1, model_width), jnp.float32)], axis=0)
    grad_dispatch = jnp.sum(
        padded_back[slot_dest.reshape(-1)].reshape(row_count, TOP, model_width), axis=1
    )
    expert_ids = jnp.arange(EXPERTS, dtype=jnp.int32)
    grad_probs = jnp.sum(
        jnp.where(route_rows[:, :, None] == expert_ids[None, None, :], grad_gate[:, :, None], 0.0),
        axis=1,
    )
    grad_logits = (
        gate_probs * (grad_probs - jnp.sum(grad_probs * gate_probs, axis=-1, keepdims=True))
    ).astype(jnp.bfloat16)
    grad_router = jnp.einsum("rd,re->de", moe_in, grad_logits, preferred_element_type=jnp.float32)
    grad_moe_in = grad_dispatch + jnp.einsum(
        "re,de->rd", grad_logits, w_router, preferred_element_type=jnp.float32
    )
    grad_mid_norm, grad_gain_two, grad_shift_two = norm_backward(
        grad_moe_in, normed_two, inv_two, gain_two
    )
    grad_middle = grad_total + grad_mid_norm
    grad_attn = grad_middle.astype(jnp.bfloat16)
    grad_proj = jnp.einsum("rd,re->de", attended, grad_attn, preferred_element_type=jnp.float32)
    grad_attended = jnp.einsum(
        "re,de->rd", grad_attn, w_proj, preferred_element_type=jnp.float32
    ).astype(jnp.bfloat16)
    grad_heads = grad_attended.reshape(head_shape)
    keys_again, values_again = (
        lax.all_gather(key_rows, "seq", axis=1, tiled=True),
        lax.all_gather(value_rows, "seq", axis=1, tiled=True),
    )
    key_heads = keys_again.reshape(head_shape)
    value_heads = values_again.reshape(head_shape)
    probs_again = jnp.exp(score_block(query_heads, key_heads, key_mask, score_scale) - log_total)
    grad_probs_att = jnp.einsum(
        "ishd,ithd->ihst", grad_heads, value_heads, preferred_element_type=jnp.float32
    )
    delta = jnp.sum(grad_probs_att * probs_again, axis=-1, keepdims=True)
    grad_scores = (probs_again * (grad_probs_att - delta)).astype(jnp.bfloat16)
    grad_queries = (
        jnp.einsum("ihst,ithd->ishd", grad_scores, key_heads, preferred_element_type=jnp.float32)
        * score_scale
    )
    grad_keys_full = (
        jnp.einsum("ihst,ishd->ithd", grad_scores, query_heads, preferred_element_type=jnp.float32)
        * score_scale
    )
    grad_values_full = jnp.einsum(
        "ihst,ishd->ithd",
        probs_again.astype(jnp.bfloat16),
        grad_heads,
        preferred_element_type=jnp.float32,
    )
    grad_keys, grad_values = (
        lax.psum_scatter(
            grad_keys_full.reshape(image_count, full_patches, model_width),
            "seq",
            scatter_dimension=1,
            tiled=True,
        ),
        lax.psum_scatter(
            grad_values_full.reshape(image_count, full_patches, model_width),
            "seq",
            scatter_dimension=1,
            tiled=True,
        ),
    )
    grad_packed = jnp.concatenate(
        [
            grad_queries.reshape(row_count, model_width),
            grad_keys.reshape(row_count, model_width),
            grad_values.reshape(row_count, model_width),
        ],
        axis=1,
    ).astype(jnp.bfloat16)
    grad_qkv = jnp.einsum("rd,re->de", attn_in, grad_packed, preferred_element_type=jnp.float32)
    grad_attn_in = jnp.einsum("re,de->rd", grad_packed, w_qkv, preferred_element_type=jnp.float32)
    grad_in_norm, grad_gain_one, grad_shift_one = norm_backward(
        grad_attn_in, normed_one, inv_one, gain_one
    )
    input_grad = (
        (grad_middle + grad_in_norm)
        .astype(jnp.bfloat16)
        .reshape(image_count, patch_rows, model_width)
    )
    summed = lax.psum(
        (
            grad_qkv,
            grad_proj,
            grad_router,
            grad_gain_one,
            grad_shift_one,
            grad_gain_two,
            grad_shift_two,
            stat_terms,
        ),
        ("seq", "ep"),
    )
    expert_grads = (
        lax.psum(grad_first.astype(jnp.bfloat16), "seq").astype(jnp.float32),
        lax.psum(grad_second.astype(jnp.bfloat16), "seq").astype(jnp.float32),
    )
    rms_stats = jnp.sqrt(summed[7][:3] / summed[7][3])
    return (
        output,
        input_grad,
        summed[3],
        summed[4],
        summed[0],
        summed[1],
        summed[5],
        summed[6],
        summed[2],
        expert_grads[0],
        expert_grads[1],
        rms_stats,
    )


def solution(mesh):
    in_specs = (
        P("ep", "seq", None),
        P("ep", "seq", None),
        P("ep", "seq"),
        P("ep"),
        P(),
        P(),
        P(),
        P(),
        P(),
        P(),
        P(),
        P("ep", None),
        P("ep", None),
        P("ep", "seq", None),
    )
    out_specs = (
        P("ep", "seq", None),
        P("ep", "seq", None),
        P(),
        P(),
        P(),
        P(),
        P(),
        P(),
        P(),
        P("ep", None),
        P("ep", None),
        P(),
    )
    return jax.shard_map(
        per_device, mesh=mesh, in_specs=in_specs, out_specs=out_specs, check_vma=False
    )
```

profile of v0, /device:TPU:0, one launch (start us, length us, event | category | flops | bytes accessed | tf_op | source)
XLA Modules:
  0.0 1413.0 jit_solution(5902060563627623308)
XLA Ops:
  28.5 6.5 gather_fusion
  35.0 7.7 gather_fusion.1
  50.4 4.8 reduce-window.6
  65.3 5.5 scatter_custom_fusion.1
  71.5 5.4 copy.110
  76.9 5.0 fusion.69
  81.9 5.0 copy-done.1
  90.7 9.3 all-gather.3.cloned.1.call-done
  100.0 5.3 copy.109
  105.3 8.2 fusion.37
  127.9 6.7 gather_fusion.4
  140.7 5.1 all-to-all-start
  156.2 4.6 mul.269
  160.8 5.4 scatter_custom_fusion.2
  169.5 12.0 gather_fusion.8
  184.7 7.0 gather_fusion.6
  197.8 5.3 all-to-all-start.2
  203.2 35.2 %fusion.2 = (bf16[8,4,29,3072]{3,2,0,1:T(8,128)(2,1)S(1)}, f32[4,8,29,3072]{3,2,1,0:T(8,128)}) fusion(bf16[4,3072,768,1]{2,1,3,0:T(8,128)(2,1)} %bitcast.184, bf16[8,4,29,768]{3,1,2,0:T(4,128)(2,1)} %all-to-all-done), kind=kOutput, calls=%fused_computation.24 | convolution fusion | flops 4564156416 | bytes 37404672 | tf_op jit(solution)/shard_map/secd,efd->secf/dot_general | solution.py:184
  238.3 11.5 fusion.30
  252.0 5.6 all-to-all-start.1
  257.6 13.6 fusion.8
  271.3 11.5 fusion.31
  285.0 7.3 all-to-all-done.1
  310.3 6.7 gather_fusion.5
  317.0 4.4 reshape.414
  321.4 7.5 multiply_reduce_fusion.1
  342.1 6.7 gather_fusion.7
  348.8 4.6 reshape.418
  353.4 6.0 reduce_sum.241
  359.5 5.4 fusion.41
  375.2 14.9 %multiply_reduce_fusion = (f32[3,12,144]{2,1,0:T(8,128)S(1)}, f32[3,12,144,576]{3,2,1,0:T(8,128)}) fusion(f32[3,12,144,576]{3,2,1,0:T(8,128)} %copy-done.1, f32[3,12,144]{2,1,0:T(8,128)} %log_add_fusion, bf16[3,144,12,64]{1,3,2,0:T(8,128)(2,1)} %copy.130, bf16[3,576,12,64]{1,3,2,0:T(8,128)(2,1)} %bitcast.170), kind=kOutput, calls=%fused_computation.17 | convolution fusion | flops 391158720 | bytes 27247104 | tf_op jit(solution)/shard_map/ishd,ithd->ihst/dot_general | solution.py:260
  390.1 9.9 multiply_convert_fusion
  404.7 7.5 copy.133
  412.2 9.9 fusion.25
  422.1 7.5 copy.135
  429.7 12.3 bitcast_convert_fusion
  442.0 12.1 bitcast_convert_fusion.1
  454.2 8.4 fusion.38
  478.4 61.2 %reduce-scatter.5.cloned.1.call-done = f32[3,144,768]{2,1,0:T(8,128)} async-done(((f32[3,576,768]{2,1,0:T(8,128)}), f32[3,144,768]{2,1,0:T(8,128)}) %reduce-scatter.5.cloned.1.call-update) | async-done | bytes 1327120 | tf_op jit(solution)/shard_map/reduce_scatter | solution.py:286
  541.8 6.5 fusion.42
  551.5 5.5 multiply_reduce_fusion.4
  557.0 40.4 %all-reduce.7 = (f32[768]{0:T(1024)}, f32[768]{0:T(1024)}, f32[768]{0:T(1024)}, f32[768]{0:T(1024)}, f32[4]{0:T(128)}) all-reduce(f32[768]{0:T(1024)} %get-tuple-element.17, f32[768]{0:T(1024)} %get-tuple-element.26, f32[768]{0:T(1024)S(1)} %copy-done.36, f32[768]{0:T(1024)S(1)} %copy-done.37, ...), channel_id=1, replica_groups=mesh['seq'=4,'ep'=8] {'seq','ep'}, use_global_device_ids=true, to_apply=%region_27.28 | all-reduce | flops 3076 | bytes 24608 | tf_op jit(solution)/shard_map/psum | solution.py:311
  605.1 588.1 %all-reduce.15.cloned.1.call-done = (bf16[12288,768]{1,0:T(8,128)(2,1)}, bf16[12288,768]{1,0:T(8,128)(2,1)}) async-done(((bf16[12288,768]{1,0:T(8,128)(2,1)}, bf16[12288,768]{1,0:T(8,128)(2,1)}), (bf16[12288,768]{1,0:T(8,128)(2,1)}, bf16[12288,768]{1,0:T(8,128)(2,1)})) %all-reduce.15.cloned.1.call-update) | async-done | bytes 37748752 | tf_op jit(solution)/shard_map/psum | solution.py:325
  1193.2 21.1 %convert_element_type.149 = f32[12288,768]{1,0:T(8,128)} convert(bf16[12288,768]{1,0:T(8,128)(2,1)} %get-tuple-element.36) | non-fusion elementwise | flops 9437184 | bytes 56623104 | tf_op jit(solution)/shard_map/convert_element_type | solution.py:325
  1214.2 4.6 copy-done.6
  1218.9 12.9 convert_element_type.152
  1231.8 165.5 %all-reduce.13.cloned.1.call-done = (f32[768,2304]{1,0:T(8,128)}, f32[768,768]{1,0:T(8,128)}, f32[768,32]{0,1:T(8,128)}) async-done(((f32[768,2304]{1,0:T(8,128)}, f32[768,768]{1,0:T(8,128)}, f32[768,32]{0,1:T(8,128)}), (f32[768,2304]{1,0:T(8,128)}, f32[768,768]{1,0:T(8,128)}, f32[768,32]{0,1:T(8,128)})) %all-reduce.13.cloned.1.call-update) | async-done | bytes 9535504 | tf_op jit(solution)/shard_map/psum | solution.py:311
  1397.3 6.6 copy.162
  (221 shorter events, 167.1 us)
Async XLA Ops:
  7.2 4.6 copy-start
  7.2 64.3 %all-gather.5.cloned.1.call-start = ((), (), s32[]{:S(2)}) async-start(), calls=%async_computation.7 | async-start | bytes 3317760 | tf_op jit(solution)/shard_map/all_gather | solution.py:151
  10.2 3.3 copy-start.32
  10.3 3.2 copy-start.34
  11.8 1.8 copy-start.12
  14.9 85.1 %all-gather.3.cloned.1.call-start = ((), (), s32[]{:S(2)}) async-start(), calls=%async_computation.6 | async-start | bytes 3317760 | tf_op jit(solution)/shard_map/all_gather | solution.py:152
  14.9 8.9 copy-start.31
  15.6 9.1 copy-start.44
  49.0 6.3 copy-start.43
  65.3 5.5 copy-start.39
  81.9 5.0 copy-start.1
  81.9 5.0 copy-start.17
  121.0 4.5 copy-start.23
  121.0 4.5 copy-start.42
  124.5 1.3 copy-start.19
  140.7 57.1 %all-to-all-start = ((bf16[8,4,29,768]{3,1,2,0:T(4,128)(2,1)}), bf16[8,4,29,768]{3,1,2,0:T(4,128)(2,1)}, u32[]{:S(2)}, u32[]{:S(2)}) async-start(bf16[8,4,29,768]{3,1,2,0:T(4,128)(2,1)} %copy.119), calls=%async_computation | async-start | bytes 2850816 | tf_op jit(solution)/shard_map/all_to_all | solution.py:126
  146.5 9.8 copy-start.25
  169.5 12.0 copy-start.38
  197.8 54.2 %all-to-all-start.2 = ((bf16[8,4,29,768]{3,1,2,0:T(4,128)(2,1)}), bf16[8,4,29,768]{3,1,2,0:T(4,128)(2,1)}, u32[]{:S(2)}, u32[]{:S(2)}) async-start(bf16[8,4,29,768]{3,1,2,0:T(4,128)(2,1)} %copy.124), calls=%async_computation.2 | async-start | bytes 2850816 | tf_op jit(solution)/shard_map/all_to_all | solution.py:126
  238.3 11.5 copy-start.46
  252.0 40.3 %all-to-all-start.1 = ((bf16[8,4,29,768]{3,1,2,0:T(4,128)(2,1)}), bf16[8,4,29,768]{3,1,2,0:T(4,128)(2,1)}, u32[]{:S(2)}, u32[]{:S(2)}) async-start(bf16[8,4,29,768]{3,1,2,0:T(4,128)(2,1)} %copy.121), calls=%async_computation.1 | async-start | bytes 2850816 | tf_op jit(solution)/shard_map/all_to_all | solution.py:129
  271.3 11.5 copy-start.45
  282.8 15.0 %copy-start.40 = (s32[864]{0:T(1024)S(1)}, s32[864]{0:T(1024)}, u32[]{:S(2)}) copy-start(s32[864]{0:T(1024)} %copy-done.39) | copy-start | bytes 10372
  292.3 41.4 %all-to-all-start.3 = ((bf16[8,4,29,768]{3,1,2,0:T(4,128)(2,1)}), bf16[8,4,29,768]{3,1,2,0:T(4,128)(2,1)}, u32[]{:S(2)}, u32[]{:S(2)}) async-start(bf16[8,4,29,768]{3,1,2,0:T(4,128)(2,1)} %copy.126), calls=%async_computation.3 | async-start | bytes 2850816 | tf_op jit(solution)/shard_map/all_to_all | solution.py:129
  296.6 179.5 %reduce-scatter.3.cloned.1.call-start = ((), (), s32[]{:S(2)}) async-start(), calls=%async_computation.8 | async-start | bytes 6635520 | tf_op jit(solution)/shard_map/reduce_scatter | solution.py:280
  321.4 9.9 copy-start.22
  321.4 9.9 copy-start.30
  353.4 6.0 copy-start.20
  353.4 6.0 copy-start.24
  353.4 6.0 copy-start.26
  353.4 6.0 copy-start.28
  359.4 5.5 copy-start.4
  359.4 5.4 copy-start.11
  364.9 1.7 copy-start.10
  365.4 1.1 copy-start.5
  375.2 14.9 %copy-start.16 = (f32[3,12,144]{2,1,0:T(8,128)S(1)}, f32[3,12,144]{2,1,0:T(8,128)}, u32[]{:S(2)}) copy-start(f32[3,12,144]{2,1,0:T(8,128)} %log_add_fusion) | copy-start | bytes 62212
  390.1 9.9 copy-start.9
  400.1 4.6 copy-start.2
  412.1 127.4 %reduce-scatter.5.cloned.1.call-start = ((), (), s32[]{:S(2)}) async-start(), calls=%async_computation.9 | async-start | bytes 6635520 | tf_op jit(solution)/shard_map/reduce_scatter | solution.py:286
  429.7 763.5 %all-reduce.15.cloned.1.call-start = ((), (), s32[]{:S(2)}) async-start(), calls=%async_computation.11 | async-start | bytes 75497472 | tf_op jit(solution)/shard_map/psum | solution.py:325
  454.2 943.1 %all-reduce.13.cloned.1.call-start = ((), (), s32[]{:S(2)}) async-start(), calls=%async_computation.10 | async-start | bytes 19070976 | tf_op jit(solution)/shard_map/psum | solution.py:311
  548.3 3.2 copy-start.33
  548.3 3.2 copy-start.35
  551.5 5.5 copy-start.36
  551.5 5.5 copy-start.37
  1193.2 25.7 %copy-start.6 = (bf16[12288,768]{1,0:T(8,128)(2,1)S(1)}, bf16[12288,768]{1,0:T(8,128)(2,1)}, u32[]{:S(2)}) copy-start(bf16[12288,768]{1,0:T(8,128)(2,1)} %get-tuple-element.37) | copy-start | bytes 56623108
  1397.3 6.6 copy-start.14
  1403.9 1.4 copy-start.18
  (9 other events, 6.8 us)
Sparse Core Ops, SparseCore 0:
  15.0 42.6 all-gather.4
  60.1 39.9 all-gather.2
  412.3 62.3 reduce-scatter.2
  477.5 61.9 reduce-scatter.4
  543.7 649.4 all-reduce.14
  1201.5 195.7 all-reduce.12
where the time goes:
time: 1420 us; the launch traced here: 1410 us
  waiting for transfers between devices  832 us (59%)
  local copies, waits for them, and re-layouts  215 us (15%)
  matrix products  178 us (13%)
  other arithmetic  110 us (8%)
  blocking collectives  40.4 us (3%)
  starting transfers between devices  20.5 us (1%)
  between operations  16.3 us (1%)
    psum x1, waiting for transfers between devices, per_device(): lax.psum(grad_first.astype(jnp.bfloat16), 'seq').astype(jnp.float32)  588 us
    psum x1, waiting for transfers between devices, per_device(): lax.psum((grad_qkv, grad_proj, grad_router, grad_gain_one, grad_shift_one...  165 us
    reduce_scatter x1, waiting for transfers between devices, per_device(): lax.psum_scatter(grad_values_full.reshape(image_count, full_patches, mode...  61.2 us
    psum x1, blocking collectives, per_device(): lax.psum((grad_qkv, grad_proj, grad_router, grad_gain_one, grad_shift_one...  40.4 us
    dot_general x1, matrix products, per_device(): jnp.einsum('secd,efd->secf', arrived, w_first, preferred_element_type=jnp...  35.2 us
  transfers between devices with their start and end apart: 10, of which 5 were waited for; matrix products, arithmetic and copies ran while one was open for 25% of the time, Pallas kernels for 0%

commit v1 on v0

--- a/solution.py
+++ b/solution.py
@@ -2,6 +2,7 @@
 import jax.numpy as jnp
 from jax import lax
 from jax.sharding import PartitionSpec as P
+from jax.lax import all_gather
 
 HEADS = 12
 EXPERTS = 32
@@ -10,6 +11,10 @@
 SHORT = 196
 norm_eps = 1e-06
 neg_big = -1e30
+
+
+def advance_clusters_for(a0):
+    return jnp.sum(all_gather(a0, "seq"), 0)
 
 
 def norm_forward(values, norm_gain, norm_bias):
@@ -322,7 +327,7 @@
         ("seq", "ep"),
     )
     expert_grads = (
-        lax.psum(grad_first.astype(jnp.bfloat16), "seq").astype(jnp.float32),
+        advance_clusters_for(grad_first.astype(jnp.bfloat16)).astype(jnp.float32),
         lax.psum(grad_second.astype(jnp.bfloat16), "seq").astype(jnp.float32),
     )
     rms_stats = jnp.sqrt(summed[7][:3] / summed[7][3])

time: 1420 us -> 1760 us (1.24)
  waiting for transfers between devices: 832 us -> 1130 us
  other arithmetic: 110 us -> 158 us
    all_gather x0 -> x1, waiting for transfers between devices: none -> 627 us  [advance_clusters_for(): return jnp.sum(all_gather(a0, 'seq'), 0)]
    psum x1, waiting for transfers between devices: 588 us -> 281 us  [per_device(): lax.psum(grad_second.astype(jnp.bfloat16), 'seq').astype(jnp.float32)]
    reduce_sum x0 -> x1, other arithmetic: none -> 36.7 us  [advance_clusters_for(): return jnp.sum(all_gather(a0, 'seq'), 0)]
    psum x1, waiting for transfers between devices: 165 us -> 144 us  [per_device(): lax.psum((grad_qkv, grad_proj, grad_router, grad_gain_one, grad_shift_one...]
  transfers between devices with their start and end apart: 10 -> 11, of which waited for: 5 -> 6; matrix products, arithmetic and copies ran while one was open for 25% -> 23% of each run, Pallas kernels for 0% -> 0%
where the time goes in v1:
time: 1760 us
  waiting for transfers between devices  1130 us (64%)
  local copies, waits for them, and re-layouts  210 us (12%)
  matrix products  178 us (10%)
  other arithmetic  158 us (9%)
  blocking collectives  40.7 us (2%)
  starting transfers between devices  20.6 us (1%)
    all_gather x1, waiting for transfers between devices, advance_clusters_for(): return jnp.sum(all_gather(a0, 'seq'), 0)  627 us
    psum x1, waiting for transfers between devices, per_device(): lax.psum(grad_second.astype(jnp.bfloat16), 'seq').astype(jnp.float32)  281 us
    psum x1, waiting for transfers between devices, per_device(): lax.psum((grad_qkv, grad_proj, grad_router, grad_gain_one, grad_shift_one...  144 us
    reduce_scatter x1, waiting for transfers between devices, per_device(): lax.psum_scatter(grad_values_full.reshape(image_count, full_patches, mode...  61.1 us
    psum x1, blocking collectives, per_device(): lax.psum((grad_qkv, grad_proj, grad_router, grad_gain_one, grad_shift_one...  40.7 us
    reduce_sum x1, other arithmetic, advance_clusters_for(): return jnp.sum(all_gather(a0, 'seq'), 0)  36.7 us
  transfers between devices with their start and end apart: 11, of which 6 were waited for; matrix products, arithmetic and copies ran while one was open for 23% of the time, Pallas kernels for 0%

profile of v1, /device:TPU:0, one launch (start us, length us, event | category | flops | bytes accessed | tf_op | source)
XLA Modules:
  0.0 1755.6 jit_solution(6469078707572773108)
XLA Ops:
  28.5 6.5 gather_fusion
  35.1 7.7 gather_fusion.1
  50.5 4.8 reduce-window.6
  65.3 5.5 scatter_custom_fusion.1
  71.6 5.4 copy.110
  77.0 5.0 fusion.69
  82.0 5.0 copy-done.1
  90.8 9.2 all-gather.4.cloned.1.call-done
  100.0 5.3 copy.109
  105.3 8.2 fusion.37
  127.9 6.7 gather_fusion.4
  140.7 5.1 all-to-all-start
  156.3 4.6 mul.269
  160.9 5.4 scatter_custom_fusion.2
  169.6 12.0 gather_fusion.8
  184.8 7.0 gather_fusion.6
  197.9 5.3 all-to-all-start.2
  203.2 35.2 %fusion.2 = (bf16[8,4,29,3072]{3,2,0,1:T(8,128)(2,1)S(1)}, f32[4,8,29,3072]{3,2,1,0:T(8,128)}) fusion(bf16[4,3072,768,1]{2,1,3,0:T(8,128)(2,1)} %bitcast.184, bf16[8,4,29,768]{3,1,2,0:T(4,128)(2,1)} %all-to-all-done), kind=kOutput, calls=%fused_computation.24 | convolution fusion | flops 4564156416 | bytes 37404672 | tf_op jit(solution)/shard_map/secd,efd->secf/dot_general | solution.py:189
  238.4 11.5 fusion.30
  252.1 5.6 all-to-all-start.1
  257.7 13.6 fusion.8
  271.3 11.5 fusion.31
  285.0 7.3 all-to-all-done.1
  310.4 6.7 gather_fusion.5
  321.5 7.5 multiply_reduce_fusion.1
  342.2 6.7 gather_fusion.7
  348.9 4.6 reshape.428
  353.5 6.0 reduce_sum.253
  359.5 5.4 fusion.41
  375.2 14.9 multiply_reduce_fusion
  390.2 9.9 multiply_convert_fusion
  404.7 7.5 copy.133
  412.3 9.9 fusion.25
  422.2 7.5 copy.135
  429.8 12.3 bitcast_convert_fusion
  442.1 12.1 bitcast_convert_fusion.1
  454.4 8.5 fusion.38
  478.5 61.1 %reduce-scatter.5.cloned.1.call-done = f32[3,144,768]{2,1,0:T(8,128)} async-done(((f32[3,576,768]{2,1,0:T(8,128)}), f32[3,144,768]{2,1,0:T(8,128)}) %reduce-scatter.5.cloned.1.call-update) | async-done | bytes 1327120 | tf_op jit(solution)/shard_map/reduce_scatter | solution.py:291
  541.8 6.5 fusion.42
  551.5 5.5 multiply_reduce_fusion.4
  557.0 40.7 %all-reduce.7 = (f32[768]{0:T(1024)}, f32[768]{0:T(1024)}, f32[768]{0:T(1024)}, f32[768]{0:T(1024)}, f32[4]{0:T(128)}) all-reduce(f32[768]{0:T(1024)} %get-tuple-element.17, f32[768]{0:T(1024)} %get-tuple-element.26, f32[768]{0:T(1024)S(1)} %copy-done.35, f32[768]{0:T(1024)S(1)} %copy-done.36, ...), channel_id=1, replica_groups=mesh['seq'=4,'ep'=8] {'seq','ep'}, use_global_device_ids=true, to_apply=%region_27.28 | all-reduce | flops 3076 | bytes 24608 | tf_op jit(solution)/shard_map/psum | solution.py:316
  605.3 281.5 %all-reduce.12.cloned.1.call-done = bf16[12288,768]{1,0:T(8,128)(2,1)} async-done(((bf16[12288,768]{1,0:T(8,128)(2,1)}), bf16[12288,768]{1,0:T(8,128)(2,1)}) %all-reduce.12.cloned.1.call-update) | async-done | bytes 18874384 | tf_op jit(solution)/shard_map/psum | solution.py:331
  886.7 24.0 %convert_element_type.161 = f32[12288,768]{1,0:T(8,128)} convert(bf16[12288,768]{1,0:T(8,128)(2,1)} %all-reduce.12.cloned.1.call-done) | non-fusion elementwise | flops 9437184 | bytes 56623104 | tf_op jit(solution)/shard_map/convert_element_type | solution.py:331
  910.7 627.0 %all-gather.8.cloned.1.call-done = bf16[4,12288,768]{2,1,0:T(8,128)(2,1)} async-done(((bf16[1,12288,768]{2,1,0:T(8,128)(2,1)}), bf16[4,12288,768]{2,1,0:T(8,128)(2,1)}) %all-gather.8.cloned.1.call-update) | async-done | bytes 75497488 | tf_op jit(solution)/shard_map/all_gather | solution.py:17
  1537.7 36.7 %reduce_sum.266 = bf16[12288,768]{1,0:T(8,128)(2,1)} reduce(bf16[4,12288,768]{2,1,0:T(8,128)(2,1)} %all-gather.8.cloned.1.call-done, bf16[]{:T(256)} %constant.69.clone.1), dimensions={0}, to_apply=%region_37.38 | reduce | flops 28311552 | bytes 94371840 | tf_op jit(solution)/shard_map/reduce_sum | solution.py:17
  1574.4 21.0 %convert_element_type.158 = f32[12288,768]{1,0:T(8,128)} convert(bf16[12288,768]{1,0:T(8,128)(2,1)} %reduce_sum.266) | non-fusion elementwise | flops 9437184 | bytes 56623104 | tf_op jit(solution)/shard_map/convert_element_type | solution.py:330
  1595.4 144.2 %all-reduce.14.cloned.1.call-done = (f32[768,2304]{1,0:T(8,128)}, f32[768,768]{1,0:T(8,128)}, f32[768,32]{0,1:T(8,128)}) async-done(((f32[768,2304]{1,0:T(8,128)}, f32[768,768]{1,0:T(8,128)}, f32[768,32]{0,1:T(8,128)}), (f32[768,2304]{1,0:T(8,128)}, f32[768,768]{1,0:T(8,128)}, f32[768,32]{0,1:T(8,128)})) %all-reduce.14.cloned.1.call-update) | async-done | bytes 9535504 | tf_op jit(solution)/shard_map/psum | solution.py:316
  1739.7 6.6 copy.161
  (223 shorter events, 171.5 us)
Async XLA Ops:
  7.2 4.6 copy-start
  7.2 64.4 %all-gather.6.cloned.1.call-start = ((), (), s32[]{:S(2)}) async-start(), calls=%async_computation.7 | async-start | bytes 3317760 | tf_op jit(solution)/shard_map/all_gather | solution.py:156
  10.2 3.3 copy-start.31
  10.3 3.2 copy-start.33
  11.8 1.8 copy-start.11
  14.9 85.1 %all-gather.4.cloned.1.call-start = ((), (), s32[]{:S(2)}) async-start(), calls=%async_computation.6 | async-start | bytes 3317760 | tf_op jit(solution)/shard_map/all_gather | solution.py:157
  14.9 8.9 copy-start.30
  15.6 9.1 copy-start.43
  49.0 6.3 copy-start.42
  65.3 5.5 copy-start.38
  81.9 5.0 copy-start.1
  81.9 5.0 copy-start.16
  121.0 4.5 copy-start.22
  121.0 4.5 copy-start.41
  124.5 1.3 copy-start.18
  140.7 57.2 %all-to-all-start = ((bf16[8,4,29,768]{3,1,2,0:T(4,128)(2,1)}), bf16[8,4,29,768]{3,1,2,0:T(4,128)(2,1)}, u32[]{:S(2)}, u32[]{:S(2)}) async-start(bf16[8,4,29,768]{3,1,2,0:T(4,128)(2,1)} %copy.119), calls=%async_computation | async-start | bytes 2850816 | tf_op jit(solution)/shard_map/all_to_all | solution.py:131
  146.5 9.8 copy-start.24
  169.6 12.0 copy-start.37
  197.9 54.2 %all-to-all-start.2 = ((bf16[8,4,29,768]{3,1,2,0:T(4,128)(2,1)}), bf16[8,4,29,768]{3,1,2,0:T(4,128)(2,1)}, u32[]{:S(2)}, u32[]{:S(2)}) async-start(bf16[8,4,29,768]{3,1,2,0:T(4,128)(2,1)} %copy.124), calls=%async_computation.2 | async-start | bytes 2850816 | tf_op jit(solution)/shard_map/all_to_all | solution.py:131
  238.4 11.5 copy-start.45
  252.1 40.3 %all-to-all-start.1 = ((bf16[8,4,29,768]{3,1,2,0:T(4,128)(2,1)}), bf16[8,4,29,768]{3,1,2,0:T(4,128)(2,1)}, u32[]{:S(2)}, u32[]{:S(2)}) async-start(bf16[8,4,29,768]{3,1,2,0:T(4,128)(2,1)} %copy.121), calls=%async_computation.1 | async-start | bytes 2850816 | tf_op jit(solution)/shard_map/all_to_all | solution.py:134
  271.3 11.5 copy-start.44
  282.8 15.0 copy-start.39
  292.4 41.3 %all-to-all-start.3 = ((bf16[8,4,29,768]{3,1,2,0:T(4,128)(2,1)}), bf16[8,4,29,768]{3,1,2,0:T(4,128)(2,1)}, u32[]{:S(2)}, u32[]{:S(2)}) async-start(bf16[8,4,29,768]{3,1,2,0:T(4,128)(2,1)} %copy.126), calls=%async_computation.3 | async-start | bytes 2850816 | tf_op jit(solution)/shard_map/all_to_all | solution.py:134
  296.7 179.6 %reduce-scatter.3.cloned.1.call-start = ((), (), s32[]{:S(2)}) async-start(), calls=%async_computation.8 | async-start | bytes 6635520 | tf_op jit(solution)/shard_map/reduce_scatter | solution.py:285
  321.5 9.9 copy-start.21
  321.5 9.9 copy-start.29
  353.5 6.0 copy-start.19
  353.5 6.0 copy-start.23
  353.5 6.0 copy-start.25
  353.5 6.0 copy-start.27
  359.5 5.5 copy-start.4
  359.5 5.4 copy-start.10
  364.9 1.7 copy-start.9
  365.5 1.1 copy-start.5
  375.2 14.9 copy-start.15
  390.2 9.9 copy-start.8
  400.1 4.6 copy-start.2
  412.2 127.4 %reduce-scatter.5.cloned.1.call-start = ((), (), s32[]{:S(2)}) async-start(), calls=%async_computation.9 | async-start | bytes 6635520 | tf_op jit(solution)/shard_map/reduce_scatter | solution.py:291
  429.7 457.0 %all-reduce.12.cloned.1.call-start = ((), (), s32[]{:S(2)}) async-start(), calls=%async_computation.11 | async-start | bytes 37748736 | tf_op jit(solution)/shard_map/psum | solution.py:331
  442.1 1095.6 %all-gather.8.cloned.1.call-start = ((), (), s32[]{:S(2)}) async-start(), calls=%async_computation.10 | async-start | bytes 94371840 | tf_op jit(solution)/shard_map/all_gather | solution.py:17
  454.3 1285.3 %all-reduce.14.cloned.1.call-start = ((), (), s32[]{:S(2)}) async-start(), calls=%async_computation.12 | async-start | bytes 19070976 | tf_op jit(solution)/shard_map/psum | solution.py:316
  548.3 3.2 copy-start.32
  548.3 3.2 copy-start.34
  551.5 5.5 copy-start.35
  551.5 5.5 copy-start.36
  1739.7 6.6 copy-start.13
  1746.2 1.4 copy-start.17
  (9 other events, 6.8 us)
Sparse Core Ops, SparseCore 0:
  15.0 42.6 all-gather.5
  60.1 39.9 all-gather.3
  412.3 62.3 reduce-scatter.2
  477.5 61.9 reduce-scatter.4
  543.5 343.1 all-reduce.11
  889.2 648.4 all-gather.7
  1546.2 193.4 all-reduce.13
